TPU v7x, 32 devices: a whole 2x2x4 slice. The times are simulated.
32 devices in a mesh: blk: 16 (over z, y, core), tp: 2 (over x).
Axes of the slice: x: 2, y: 2, z: 4, core: 2. Of those that a mesh axis runs over, the one named last changes fastest.
Arguments:
- frames: bfloat16 [4096, 1024], P('blk'), may hold values from -6 to 6
- clip_lengths: int32 [8], replicated, may hold values from 1 to 3841, 4096 in all
- text_states: bfloat16 [128, 1024], replicated, may hold values from -6 to 6
- text_segments: int32 [128], replicated, may hold values from 0 to 7, never falling along the last dimension, each value on 1 to 32 neighbouring positions
- gain_one: float32 [1024], replicated, may hold values from 0.1 to 1.9
- shift_one: float32 [1024], replicated, may hold values from -1.5 to 1.5
- gain_two: float32 [1024], replicated, may hold values from 0.1 to 1.9
- shift_two: float32 [1024], replicated, may hold values from -1.5 to 1.5
- gain_three: float32 [1024], replicated, may hold values from 0.1 to 1.9
- shift_three: float32 [1024], replicated, may hold values from -1.5 to 1.5
- query_weight: bfloat16 [1024, 1024], P(None, 'tp'), may hold values from -0.1875 to 0.1875
- key_weight: bfloat16 [1024, 1024], P(None, 'tp'), may hold values from -0.1875 to 0.1875
- value_weight: bfloat16 [1024, 1024], P(None, 'tp'), may hold values from -0.1875 to 0.1875
- output_weight: bfloat16 [1024, 1024], P('tp'), may hold values from -0.75 to 0.75
- cross_query: bfloat16 [1024, 1024], P(None, 'tp'), may hold values from -0.1875 to 0.1875
- cross_key: bfloat16 [1024, 1024], P(None, 'tp'), may hold values from -0.1875 to 0.1875
- cross_value: bfloat16 [1024, 1024], P(None, 'tp'), may hold values from -0.1875 to 0.1875
- cross_output: bfloat16 [1024, 1024], P('tp'), may hold values from -0.375 to 0.375
- inner_weight: bfloat16 [1024, 4096], P(None, 'tp'), may hold values from -0.1875 to 0.1875
- outer_weight: bfloat16 [4096, 1024], P('tp'), may hold values from -0.09375 to 0.09375
- cotangent: bfloat16 [4096, 1024], P('blk'), may hold values from -6 to 6
Outputs:
- result: bfloat16 [4096, 1024], P('blk')
- grad_frames: bfloat16 [4096, 1024], P('blk')
- grad_text: float32 [128, 1024], replicated
- grad_gain_one: float32 [1024], replicated
- grad_shift_one: float32 [1024], replicated
- grad_gain_two: float32 [1024], replicated
- grad_shift_two: float32 [1024], replicated
- grad_gain_three: float32 [1024], replicated
- grad_shift_three: float32 [1024], replicated
- grad_query_weight: float32 [1024, 1024], P(None, 'tp')
- grad_key_weight: float32 [1024, 1024], P(None, 'tp')
- grad_value_weight: float32 [1024, 1024], P(None, 'tp')
- grad_output_weight: float32 [1024, 1024], P('tp')
- grad_cross_query: float32 [1024, 1024], P(None, 'tp')
- grad_cross_key: float32 [1024, 1024], P(None, 'tp')
- grad_cross_value: float32 [1024, 1024], P(None, 'tp')
- grad_cross_output: float32 [1024, 1024], P('tp')
- grad_inner_weight: float32 [1024, 4096], P(None, 'tp')
- grad_outer_weight: float32 [4096, 1024], P('tp')
Inputs may be any that keep to these rules, and one draw needn't show every extreme that they name: `clip_lengths`: clips follow one another in the pack; one of them has 3841 frames. `text_segments`: text tokens of a clip stand together and in clip order; every clip has 1 to 32 of them, one exactly 32.
All inputs are finite; a program needn't handle non-finite values.
Results may differ from a plain program's by a relative error of at most 0.028.
Values may be sent and summed in bfloat16 or wider, within the bound.
No kernel may reach another device: no remote copies, remote signals or barrier semaphores. Data moves between devices by JAX's collectives and lax.ppermute only.
A program may use at most 384 MiB of HBM per device.

v0:
```python
import jax
import jax.numpy as jnp
from jax import lax
from jax.sharding import PartitionSpec as P

HEAD_DIM = 64
EPSILON = 1e-05
NEGATIVE = -1e30


def shifted(block, axis, distance):
    devices = range(lax.axis_size(axis))
    route = [(i - distance, i) for i in devices if i - distance in devices]
    return lax.ppermute(block, axis, route)


def shifted_2(value, axis, by):
    size = lax.axis_size(axis)
    return lax.ppermute(value, axis, [(i, (i + by) % size) for i in range(size)])


def layer_norm(values, gain, shift):
    centre = values - jnp.mean(values, axis=-1, keepdims=True)
    spread = jnp.mean(centre * centre, axis=-1, keepdims=True)
    return centre * lax.rsqrt(spread + EPSILON) * gain + shift


def norm_grads(values, gain, shift, grad):
    _, pullback = jax.vjp(layer_norm, values, gain, shift)
    return pullback(grad)


def gelu_exact(values):
    return jax.nn.gelu(values, approximate=False)


def clip_rows(positions, clip_lengths):
    ends = jnp.cumsum(clip_lengths)
    starts = ends - clip_lengths
    segment = jnp.sum((positions[:, None] >= ends[None, :]).astype(jnp.int32), axis=1)
    match = segment[:, None] == jnp.arange(clip_lengths.shape[0], dtype=jnp.int32)[None, :]
    first = jnp.sum(jnp.where(match, starts[None, :], 0), axis=1)
    return (segment, first)


def matmul(left, right):
    return jnp.dot(left, right, preferred_element_type=jnp.float32)


def head_sum(values):
    return lax.psum(values.astype(jnp.bfloat16), "tp").astype(jnp.float32)


def unchanged(state):
    return state


def block_grads(
    query_heads,
    grad_heads,
    log_total,
    delta,
    query_rows,
    query_first,
    key_heads,
    value_heads,
    key_rows,
):
    allowed = (key_rows[None, :] <= query_rows[:, None]) & (
        key_rows[None, :] >= query_first[:, None]
    )
    score = jnp.einsum("qhd,khd->hqk", query_heads, key_heads, preferred_element_type=jnp.float32)
    weights = jnp.exp(jnp.where(allowed[None], score - log_total[:, :, None], NEGATIVE))
    grad_weights = jnp.einsum(
        "qhd,khd->hqk", grad_heads, value_heads, preferred_element_type=jnp.float32
    )
    grad_score = (weights * (grad_weights - delta[:, :, None])).astype(jnp.bfloat16)
    query_part = jnp.einsum(
        "hqk,khd->qhd", grad_score, key_heads, preferred_element_type=jnp.float32
    )
    key_part = jnp.einsum(
        "hqk,qhd->khd", grad_score, query_heads, preferred_element_type=jnp.float32
    )
    value_part = jnp.einsum(
        "hqk,qhd->khd", weights.astype(jnp.bfloat16), grad_heads, preferred_element_type=jnp.float32
    )
    return (query_part, key_part, value_part)


def shards(
    frames,
    clip_lengths,
    text_states,
    text_segments,
    gain_one,
    shift_one,
    gain_two,
    shift_two,
    gain_three,
    shift_three,
    query_weight,
    key_weight,
    value_weight,
    output_weight,
    cross_query,
    cross_key,
    cross_value,
    cross_output,
    inner_weight,
    outer_weight,
    cotangent,
):
    row_count = frames.shape[0]
    text_count = text_states.shape[0]
    width_here = query_weight.shape[1]
    heads_here = width_here // HEAD_DIM
    blk_count = lax.axis_size("blk")
    blk_index = lax.axis_index("blk")
    scale = float(HEAD_DIM) ** (-0.5)
    my_first_row = blk_index * row_count
    offsets = jnp.arange(row_count, dtype=jnp.int32)
    rows = my_first_row + offsets
    segment, first = clip_rows(rows, clip_lengths)
    inputs = frames.astype(jnp.float32)
    normed_one = layer_norm(inputs, gain_one, shift_one).astype(jnp.bfloat16)
    queries = (matmul(normed_one, query_weight) * scale).astype(jnp.bfloat16)
    keys = matmul(normed_one, key_weight).astype(jnp.bfloat16)
    values = matmul(normed_one, value_weight).astype(jnp.bfloat16)
    query_heads = queries.reshape(row_count, heads_here, HEAD_DIM)
    start_state = (
        jnp.zeros((row_count, heads_here, HEAD_DIM), jnp.float32),
        jnp.full((heads_here, row_count), NEGATIVE, jnp.float32),
        jnp.zeros((heads_here, row_count), jnp.float32),
    )
    start = jnp.int32(0)
    key_piece = lax.all_gather(keys, "blk", axis=0, tiled=True)
    value_piece = lax.all_gather(values, "blk", axis=0, tiled=True)
    count = key_piece.shape[0]
    key_rows = jnp.arange(count, dtype=jnp.int32)

    def fold_work(state):
        totals, run_max, run_sum = state
        piece_keys = key_piece.reshape(count, heads_here, HEAD_DIM)
        piece_values = value_piece.reshape(count, heads_here, HEAD_DIM)
        score = jnp.einsum(
            "qhd,khd->hqk", query_heads, piece_keys, preferred_element_type=jnp.float32
        )
        allowed = (key_rows[None, :] <= rows[:, None]) & (key_rows[None, :] >= first[:, None])
        masked = jnp.where(allowed[None], score, NEGATIVE)
        new_max = jnp.maximum(run_max, jnp.max(masked, axis=-1))
        expo = jnp.where(allowed[None], jnp.exp(masked - new_max[:, :, None]), 0.0)
        run_sum = jnp.sum(expo, axis=-1)
        added = jnp.einsum(
            "hqk,khd->qhd",
            expo.astype(jnp.bfloat16),
            piece_values,
            preferred_element_type=jnp.float32,
        )
        totals = added
        return (totals, new_max, run_sum)

    needed = (start <= rows[-1]) & (start + count - 1 >= first[0])
    totals, run_max, run_sum = lax.cond(needed, fold_work, unchanged, start_state)
    self_out = totals / jnp.transpose(run_sum)[:, :, None]
    log_total = run_max + jnp.log(run_sum)
    attended = self_out.reshape(row_count, width_here).astype(jnp.bfloat16)
    first_sum = inputs + head_sum(matmul(attended, output_weight))
    normed_two = layer_norm(first_sum, gain_two, shift_two).astype(jnp.bfloat16)
    cross_queries = (matmul(normed_two, cross_query) * scale).astype(jnp.bfloat16)
    text_keys = matmul(text_states, cross_key).astype(jnp.bfloat16)
    text_values = matmul(text_states, cross_value).astype(jnp.bfloat16)
    cross_heads = cross_queries.reshape(row_count, heads_here, HEAD_DIM)
    text_key_heads = text_keys.reshape(text_count, heads_here, HEAD_DIM)
    text_value_heads = text_values.reshape(text_count, heads_here, HEAD_DIM)
    allowed_text = segment[:, None] == text_segments[None, :]
    cross_score = jnp.einsum(
        "qhd,khd->hqk", cross_heads, text_key_heads, preferred_element_type=jnp.float32
    )
    cross_masked = jnp.where(allowed_text[None], cross_score, NEGATIVE)
    cross_max = jnp.max(cross_masked, axis=-1, keepdims=True)
    cross_expo = jnp.where(allowed_text[None], jnp.exp(cross_masked - cross_max), 0.0)
    cross_weights = cross_expo / jnp.sum(cross_expo, axis=-1, keepdims=True)
    cross_weights_low = cross_weights.astype(jnp.bfloat16)
    cross_out = jnp.einsum(
        "hqk,khd->qhd", cross_weights_low, text_value_heads, preferred_element_type=jnp.float32
    )
    crossed = cross_out.reshape(row_count, width_here).astype(jnp.bfloat16)
    second_sum = first_sum + head_sum(matmul(crossed, cross_output))
    normed_three = layer_norm(second_sum, gain_three, shift_three).astype(jnp.bfloat16)
    hidden_pre = matmul(normed_three, inner_weight)
    hidden = gelu_exact(hidden_pre).astype(jnp.bfloat16)
    output = second_sum + head_sum(matmul(hidden, outer_weight))
    grad_output = cotangent.astype(jnp.float32)
    grad_outer = matmul(hidden.T, cotangent)
    grad_hidden = matmul(cotangent, outer_weight.T)
    _, gelu_back = jax.vjp(gelu_exact, hidden_pre)
    grad_pre = gelu_back(grad_hidden)[0].astype(jnp.bfloat16)
    grad_inner = matmul(normed_three.T, grad_pre)
    grad_normed_three = head_sum(matmul(grad_pre, inner_weight.T))
    through_three, grad_gain_three, grad_shift_three = norm_grads(
        second_sum, gain_three, shift_three, grad_normed_three
    )
    grad_second = grad_output + through_three
    grad_second_low = grad_second.astype(jnp.bfloat16)
    grad_cross_output = matmul(crossed.T, grad_second_low)
    grad_crossed = (
        matmul(grad_second_low, cross_output.T)
        .astype(jnp.bfloat16)
        .reshape(row_count, heads_here, HEAD_DIM)
    )
    grad_cross_weights = jnp.einsum(
        "qhd,khd->hqk", grad_crossed, text_value_heads, preferred_element_type=jnp.float32
    )
    cross_delta = jnp.transpose(jnp.sum(grad_crossed.astype(jnp.float32) * cross_out, axis=-1))
    grad_cross_score = (cross_weights * (grad_cross_weights - cross_delta[:, :, None])).astype(
        jnp.bfloat16
    )
    grad_cross_heads = jnp.einsum(
        "hqk,khd->qhd", grad_cross_score, text_key_heads, preferred_element_type=jnp.float32
    ).astype(jnp.bfloat16)
    grad_cross_queries = (grad_cross_heads * scale).reshape(row_count, width_here)
    text_key_part = jnp.einsum(
        "hqk,qhd->khd", grad_cross_score, cross_heads, preferred_element_type=jnp.float32
    )
    text_value_part = jnp.einsum(
        "hqk,qhd->khd", cross_weights_low, grad_crossed, preferred_element_type=jnp.float32
    )
    grad_text_keys, grad_text_values = lax.psum(
        (
            text_key_part.reshape(text_count, width_here),
            text_value_part.reshape(text_count, width_here),
        ),
        "blk",
    )
    grad_text_keys = grad_text_keys.astype(jnp.bfloat16)
    grad_text_values = grad_text_values.astype(jnp.bfloat16)
    grad_cross_key = matmul(text_states.T, grad_text_keys)
    grad_cross_value = matmul(text_states.T, grad_text_values)
    grad_text = lax.psum(
        (matmul(grad_text_keys, cross_key.T) + matmul(grad_text_values, cross_value.T)).astype(
            jnp.bfloat16
        ),
        "tp",
    ).astype(jnp.float32)
    grad_cross_query = matmul(normed_two.T, grad_cross_queries)
    grad_normed_two = head_sum(matmul(grad_cross_queries, cross_query.T))
    through_two, grad_gain_two, grad_shift_two = norm_grads(
        first_sum, gain_two, shift_two, grad_normed_two
    )
    grad_first = grad_second + through_two
    grad_first_low = grad_first.astype(jnp.bfloat16)
    grad_output_weight = matmul(attended.T, grad_first_low)
    grad_attended = matmul(grad_first_low, output_weight.T).astype(jnp.bfloat16)
    grad_heads = grad_attended.reshape(row_count, heads_here, HEAD_DIM)
    self_delta = jnp.transpose(jnp.sum(grad_heads.astype(jnp.float32) * self_out, axis=-1))
    zero_block = jnp.zeros((row_count, width_here), jnp.float32)

    def key_turn(turn, carry):
        source = (blk_index - turn) % blk_count
        base = source * row_count

        def key_work(state):
            key_block, value_block, key_grad, value_grad, query_grad = state
            query_part, key_part, value_part = block_grads(
                query_heads,
                grad_heads,
                log_total,
                self_delta,
                rows,
                first,
                key_block.reshape(row_count, heads_here, HEAD_DIM),
                value_block.reshape(row_count, heads_here, HEAD_DIM),
                base + offsets,
            )
            return (
                key_block,
                value_block,
                key_grad + key_part.reshape(row_count, width_here),
                value_grad + value_part.reshape(row_count, width_here),
                query_grad + query_part.reshape(row_count, width_here),
            )

        needed = (base <= rows[-1]) & (base + row_count - 1 >= first[0])
        key_block, value_block, key_grad, value_grad, query_grad = lax.cond(
            needed, key_work, unchanged, carry
        )
        key_block, value_block = shifted((key_block, value_block), "blk", 1)
        key_grad, value_grad = (
            shifted_2(key_grad.astype(jnp.bfloat16), "blk", 1).astype(key_grad.dtype),
            shifted_2(value_grad.astype(jnp.bfloat16), "blk", 1).astype(value_grad.dtype),
        )
        return (key_block, value_block, key_grad, value_grad, query_grad)

    final = lax.fori_loop(
        0, blk_count, key_turn, (keys, values, zero_block, zero_block, zero_block)
    )
    key_total, value_total, query_total = (final[2], final[3], final[4])
    grad_queries = query_total.astype(jnp.bfloat16) * scale
    grad_keys = key_total.astype(jnp.bfloat16)
    grad_values = value_total.astype(jnp.bfloat16)
    grad_query_weight = matmul(normed_one.T, grad_queries)
    grad_key_weight = matmul(normed_one.T, grad_keys)
    grad_value_weight = matmul(normed_one.T, grad_values)
    grad_normed_one = head_sum(
        matmul(grad_queries, query_weight.T)
        + matmul(grad_keys, key_weight.T)
        + matmul(grad_values, value_weight.T)
    )
    through_one, grad_gain_one, grad_shift_one = norm_grads(
        inputs, gain_one, shift_one, grad_normed_one
    )
    grad_frames = (grad_first + through_one).astype(jnp.bfloat16)
    (
        grad_query_weight,
        grad_key_weight,
        grad_value_weight,
        grad_output_weight,
        grad_cross_query,
        grad_cross_output,
        grad_inner,
        grad_outer,
        grad_gain_one,
        grad_shift_one,
        grad_gain_two,
        grad_shift_two,
        grad_gain_three,
        grad_shift_three,
    ) = lax.psum(
        (
            grad_query_weight,
            grad_key_weight,
            grad_value_weight,
            grad_output_weight,
            grad_cross_query,
            grad_cross_output,
            grad_inner,
            grad_outer,
            grad_gain_one,
            grad_shift_one,
            grad_gain_two,
            grad_shift_two,
            grad_gain_three,
            grad_shift_three,
        ),
        "blk",
    )
    return (
        output.astype(jnp.bfloat16),
        grad_frames,
        grad_text,
        grad_gain_one,
        grad_shift_one,
        grad_gain_two,
        grad_shift_two,
        grad_gain_three,
        grad_shift_three,
        grad_query_weight,
        grad_key_weight,
        grad_value_weight,
        grad_output_weight,
        grad_cross_query,
        grad_cross_key,
        grad_cross_value,
        grad_cross_output,
        grad_inner,
        grad_outer,
    )


def solution(mesh):
    return jax.shard_map(
        shards,
        mesh=mesh,
        in_specs=(
            P("blk", None),
            P(),
            P(),
            P(),
            P(),
            P(),
            P(),
            P(),
            P(),
            P(),
            P(None, "tp"),
            P(None, "tp"),
            P(None, "tp"),
            P("tp", None),
            P(None, "tp"),
            P(None, "tp"),
            P(None, "tp"),
            P("tp", None),
            P(None, "tp"),
            P("tp", None),
            P("blk", None),
        ),
        out_specs=(
            P("blk", None),
            P("blk", None),
            P(),
            P(),
            P(),
            P(),
            P(),
            P(),
            P(),
            P(None, "tp"),
            P(None, "tp"),
            P(None, "tp"),
            P("tp", None),
            P(None, "tp"),
            P(None, "tp"),
            P(None, "tp"),
            P("tp", None),
            P(None, "tp"),
            P("tp", None),
        ),
        check_vma=False,
    )
```

profile of v0, /device:TPU:0, one launch (start us, length us, event | category | flops | bytes accessed | tf_op | source)
XLA Modules:
  0.0 1468.9 jit_solution(12834105977165518617)
XLA Ops:
  21.8 44.2 %all-gather.3.cloned.1.call-done = bf16[4096,512]{1,0:T(8,128)(2,1)} async-done(((bf16[256,512]{1,0:T(8,128)(2,1)}), bf16[4096,512]{1,0:T(8,128)(2,1)}) %all-gather.3.cloned.1.call-update) | async-done | bytes 4194320 | tf_op jit(solution)/shard_map/all_gather | solution.py:136
  66.1 51.8 %all-gather.5.cloned.1.call-done = bf16[4096,512]{1,0:T(8,128)(2,1)} async-done(((bf16[256,512]{1,0:T(8,128)(2,1)}), bf16[4096,512]{1,0:T(8,128)(2,1)}) %all-gather.5.cloned.1.call-update) | async-done | bytes 4194320 | tf_op jit(solution)/shard_map/all_gather | solution.py:137
  117.9 62.9 %conditional.2 = (f32[256,8,64]{0,2,1:T(8,128)S(1)}, f32[8,256]{1,0:T(8,128)}, f32[8,256]{1,0:T(8,128)}, f32[8,256]{1,0:T(8,128)S(1)}) conditional(s32[]{:T(128)} %bitcast.13, () %tuple.55, (s32[4096]{0:T(1024)S(1)}, s32[4096]{0:T(1024)S(1)}, s32[256]{0:T(256)}, s32[256]{0:T(256)}, bf16[4096,512]{1,0:T(8,128)(2,1)}, ...), branch_computations={%region_5.6_spmd, %region_6.9_spmd} | conditional | flops 2234513408 | bytes 130910240 | solution.py:163
  125.8 6.3 copy.80
  132.2 15.7 %select_reduce_fusion = (f32[8,256]{1,0:T(8,128)S(1)}, f32[8,256,4096]{2,1,0:T(8,128)}) fusion(pred[256,4096]{1,0:T(8,128)(4,1)S(1)} %compare_and_fusion, bf16[256,8,64]{0,2,1:T(8,128)(2,1)S(1)} %get-tuple-element.475, bf16[4096,8,64]{0,2,1:T(8,128)(2,1)} %bitcast.126), kind=kOutput, calls=%fused_computation.2 | convolution fusion | flops 1090516992 | bytes 39067648 | tf_op jit(solution)/shard_map/cond/branch_1_fun/qhd,khd->hqk/dot_general | solution.py:145
  148.4 15.5 %fusion.7 = f32[256,8,64]{0,2,1:T(8,128)S(1)} fusion(bf16[4096,8,64]{0,2,1:T(8,128)(2,1)} %bitcast.133, f32[8,256,4096]{2,1,0:T(8,128)} %get-tuple-element.768, f32[8,256]{1,0:T(8,128)} %broadcast_maximum_fusion, pred[256,4096]{1,0:T(8,128)(4,1)S(1)} %compare_and_fusion), kind=kOutput, calls=%fused_computation.8 | convolution fusion | flops 1107296256 | bytes 39329792 | tf_op jit(solution)/shard_map/cond/branch_1_fun/hqk,khd->qhd/dot_general | solution.py:153
  163.9 16.2 %fusion.2 = f32[8,256]{1,0:T(8,128)} fusion(f32[8,256,4096]{2,1,0:T(8,128)} %get-tuple-element.768, f32[8,256]{1,0:T(8,128)} %broadcast_maximum_fusion, pred[256,4096]{1,0:T(8,128)(4,1)S(1)} %compare_and_fusion), kind=kLoop, calls=%fused_computation.3 | loop fusion | flops 33552384 | bytes 34619392 | tf_op jit(solution)/shard_map/cond/branch_1_fun/reduce_sum | solution.py:152
  189.6 21.9 %all-reduce.12.cloned.1.call-done = bf16[256,1024]{1,0:T(8,128)(2,1)} async-done(((bf16[256,1024]{1,0:T(8,128)(2,1)}), bf16[256,1024]{1,0:T(8,128)(2,1)}) %all-reduce.12.cloned.1.call-update) | async-done | bytes 524304 | tf_op jit(solution)/shard_map/psum | solution.py:51
  228.4 25.3 %all-reduce.14.cloned.1.call-done = bf16[256,1024]{1,0:T(8,128)(2,1)} async-done(((bf16[256,1024]{1,0:T(8,128)(2,1)}), bf16[256,1024]{1,0:T(8,128)(2,1)}) %all-reduce.14.cloned.1.call-update) | async-done | bytes 524304 | tf_op jit(solution)/shard_map/psum | solution.py:51
  260.2 6.6 add_convert_fusion
  285.1 15.5 %all-reduce.16.cloned.1.call-done = bf16[256,1024]{1,0:T(8,128)(2,1)} async-done(((bf16[256,1024]{1,0:T(8,128)(2,1)}), bf16[256,1024]{1,0:T(8,128)(2,1)}) %all-reduce.16.cloned.1.call-update) | async-done | bytes 524304 | tf_op jit(solution)/shard_map/psum | solution.py:51
  317.8 25.6 %all-reduce.18.cloned.1.call-done = bf16[256,1024]{1,0:T(8,128)(2,1)} async-done(((bf16[256,1024]{1,0:T(8,128)(2,1)}), bf16[256,1024]{1,0:T(8,128)(2,1)}) %all-reduce.18.cloned.1.call-update) | async-done | bytes 524304 | tf_op jit(solution)/shard_map/psum | solution.py:51
  353.3 421.7 %while.26 = (s32[]{:T(128)}, bf16[256,512]{0,1:T(8,128)(2,1)S(1)}, bf16[256,512]{0,1:T(8,128)(2,1)}, f32[256,512]{0,1:T(8,128)}, f32[256,512]{0,1:T(8,128)}, /*i...) while((s32[]{:T(128)}, bf16[256,512]{0,1:T(8,128)(2,1)S(1)}, ...), condition=%wide.region_29.30_spmd.clone, body=%wide.region_26.29_spmd.clone.sunk | while | flops 341115168 | bytes 37714808 | solution.py:294
  413.3 7.3 collective-permute-start.3
  443.0 7.5 collective-permute-start
  473.5 10.1 collective-permute-start.1
  573.9 7.4 collective-permute-start
  604.4 9.1 collective-permute-start.1
  704.7 7.4 collective-permute-start
  735.2 8.1 collective-permute-start.1
  784.6 31.8 %all-reduce.20.cloned.1.call-done = bf16[256,1024]{1,0:T(8,128)(2,1)} async-done(((bf16[256,1024]{1,0:T(8,128)(2,1)}), bf16[256,1024]{1,0:T(8,128)(2,1)}) %all-reduce.20.cloned.1.call-update) | async-done | bytes 524304 | tf_op jit(solution)/shard_map/psum | solution.py:51
  820.2 67.9 %all-reduce.25 = (bf16[128,512]{0,1:T(8,128)(2,1)S(1)}, bf16[128,512]{0,1:T(8,128)(2,1)}, f32[1024]{0:T(1024)}, f32[1024]{0:T(1024)}, f32[1024]{0:T(1024)}, /*in...) all-reduce(f32[128,512]{0,1:T(8,128)S(1)} %bitcast.142, ...), channel_id=1, replica_groups=mesh['blk'=16,'tp'=2] {'blk'}, use_global_device_ids=true, to_apply=%region_33.34 | all-reduce | flops 137216 | bytes 835584 | tf_op jit(solution)/shard_map/psum | solution.py:228
  909.3 13.6 all-reduce.24.cloned.1.call-done
  926.7 512.8 %all-reduce.22.cloned.1.call-done = (f32[1024,512]{1,0:T(8,128)}, f32[1024,512]{1,0:T(8,128)}, f32[1024,512]{1,0:T(8,128)}, f32[512,1024]{1,0:T(8,128)}, f32[102...) async-done(((f32[1024,512]{1,0:T(8,128)}, f32[1024,512]{1,0:T(8,128)}, f32[1024,512]{1,0:T(8,128)}, f32[512,1024]{1,0:T(8,128)}, ...) | async-done | bytes 29360144 | tf_op jit(solution)/shard_map/psum | solution.py:328
  (720 shorter events, 506.8 us)
Async XLA Ops:
  7.3 58.8 %all-gather.3.cloned.1.call-start = ((), (), s32[]{:S(2)}) async-start(), calls=%async_computation | async-start | bytes 4456448 | tf_op jit(solution)/shard_map/all_gather | solution.py:136
  12.7 105.2 %all-gather.5.cloned.1.call-start = ((), (), s32[]{:S(2)}) async-start(), calls=%async_computation.1 | async-start | bytes 4456448 | tf_op jit(solution)/shard_map/all_gather | solution.py:137
  14.0 197.5 %all-reduce.12.cloned.1.call-start = ((), (), s32[]{:S(2)}) async-start(), calls=%async_computation.2 | async-start | bytes 1048576 | tf_op jit(solution)/shard_map/psum | solution.py:51
  184.3 69.4 %all-reduce.14.cloned.1.call-start = ((), (), s32[]{:S(2)}) async-start(), calls=%async_computation.3 | async-start | bytes 1048576 | tf_op jit(solution)/shard_map/psum | solution.py:51
  224.9 75.7 %all-reduce.16.cloned.1.call-start = ((), (), s32[]{:S(2)}) async-start(), calls=%async_computation.4 | async-start | bytes 1048576 | tf_op jit(solution)/shard_map/psum | solution.py:51
  271.9 71.5 %all-reduce.18.cloned.1.call-start = ((), (), s32[]{:S(2)}) async-start(), calls=%async_computation.5 | async-start | bytes 1048576 | tf_op jit(solution)/shard_map/psum | solution.py:51
  314.6 501.9 %all-reduce.20.cloned.1.call-start = ((), (), s32[]{:S(2)}) async-start(), calls=%async_computation.6 | async-start | bytes 1048576 | tf_op jit(solution)/shard_map/psum | solution.py:51
  410.3 17.5 %collective-permute-start.2 = (bf16[256,512]{0,1:T(8,128)(2,1)S(1)}, bf16[256,512]{0,1:T(8,128)(2,1)}, u32[]{:S(2)}, u32[]{:S(2)}) collective-permute-start(bf16[256,512]{0,1:T(8,128)(2,1)S(1)} %convert_element_type.500), channel_id=1, source_target_pairs={{0,2},{2,4},{4,6},{6,8},{8,10},{10,12},{12,14},{14,16},{16,18},{18... | collective-permute-start | bytes 786440 | tf_op jit(solution)/shard_map/while/body/eval_jaxpr/ppermute | solution.py:19
  438.2 17.5 %collective-permute-start.2 = (bf16[256,512]{0,1:T(8,128)(2,1)S(1)}, bf16[256,512]{0,1:T(8,128)(2,1)}, u32[]{:S(2)}, u32[]{:S(2)}) collective-permute-start(bf16[256,512]{0,1:T(8,128)(2,1)S(1)} %convert_element_type.500), channel_id=1, source_target_pairs={{0,2},{2,4},{4,6},{6,8},{8,10},{10,12},{12,14},{14,16},{16,18},{18... | collective-permute-start | bytes 786440 | tf_op jit(solution)/shard_map/while/body/eval_jaxpr/ppermute | solution.py:19
  440.7 16.8 %collective-permute-start.3 = (bf16[256,512]{0,1:T(8,128)(2,1)}, bf16[256,512]{0,1:T(8,128)(2,1)S(1)}, u32[]{:S(2)}, u32[]{:S(2)}) collective-permute-start(bf16[256,512]{0,1:T(8,128)(2,1)} %convert_element_type.502), channel_id=1, source_target_pairs={{0,2},{2,4},{4,6},{6,8},{8,10},{10,12},{12,14},{14,16},{16,18},{18... | collective-permute-start | bytes 786440 | tf_op jit(solution)/shard_map/while/body/eval_jaxpr/ppermute | solution.py:19
  466.1 17.5 %collective-permute-start.2 = (bf16[256,512]{0,1:T(8,128)(2,1)S(1)}, bf16[256,512]{0,1:T(8,128)(2,1)}, u32[]{:S(2)}, u32[]{:S(2)}) collective-permute-start(bf16[256,512]{0,1:T(8,128)(2,1)S(1)} %convert_element_type.500), channel_id=1, source_target_pairs={{0,2},{2,4},{4,6},{6,8},{8,10},{10,12},{12,14},{14,16},{16,18},{18... | collective-permute-start | bytes 786440 | tf_op jit(solution)/shard_map/while/body/eval_jaxpr/ppermute | solution.py:19
  468.6 16.8 %collective-permute-start.3 = (bf16[256,512]{0,1:T(8,128)(2,1)}, bf16[256,512]{0,1:T(8,128)(2,1)S(1)}, u32[]{:S(2)}, u32[]{:S(2)}) collective-permute-start(bf16[256,512]{0,1:T(8,128)(2,1)} %convert_element_type.502), channel_id=1, source_target_pairs={{0,2},{2,4},{4,6},{6,8},{8,10},{10,12},{12,14},{14,16},{16,18},{18... | collective-permute-start | bytes 786440 | tf_op jit(solution)/shard_map/while/body/eval_jaxpr/ppermute | solution.py:19
  541.2 17.5 %collective-permute-start.2 = (bf16[256,512]{0,1:T(8,128)(2,1)S(1)}, bf16[256,512]{0,1:T(8,128)(2,1)}, u32[]{:S(2)}, u32[]{:S(2)}) collective-permute-start(bf16[256,512]{0,1:T(8,128)(2,1)S(1)} %convert_element_type.500), channel_id=1, source_target_pairs={{0,2},{2,4},{4,6},{6,8},{8,10},{10,12},{12,14},{14,16},{16,18},{18... | collective-permute-start | bytes 786440 | tf_op jit(solution)/shard_map/while/body/eval_jaxpr/ppermute | solution.py:19
  543.6 16.8 %collective-permute-start.3 = (bf16[256,512]{0,1:T(8,128)(2,1)}, bf16[256,512]{0,1:T(8,128)(2,1)S(1)}, u32[]{:S(2)}, u32[]{:S(2)}) collective-permute-start(bf16[256,512]{0,1:T(8,128)(2,1)} %convert_element_type.502), channel_id=1, source_target_pairs={{0,2},{2,4},{4,6},{6,8},{8,10},{10,12},{12,14},{14,16},{16,18},{18... | collective-permute-start | bytes 786440 | tf_op jit(solution)/shard_map/while/body/eval_jaxpr/ppermute | solution.py:19
  569.1 17.4 %collective-permute-start.2 = (bf16[256,512]{0,1:T(8,128)(2,1)S(1)}, bf16[256,512]{0,1:T(8,128)(2,1)}, u32[]{:S(2)}, u32[]{:S(2)}) collective-permute-start(bf16[256,512]{0,1:T(8,128)(2,1)S(1)} %convert_element_type.500), channel_id=1, source_target_pairs={{0,2},{2,4},{4,6},{6,8},{8,10},{10,12},{12,14},{14,16},{16,18},{18... | collective-permute-start | bytes 786440 | tf_op jit(solution)/shard_map/while/body/eval_jaxpr/ppermute | solution.py:19
  571.5 16.8 %collective-permute-start.3 = (bf16[256,512]{0,1:T(8,128)(2,1)}, bf16[256,512]{0,1:T(8,128)(2,1)S(1)}, u32[]{:S(2)}, u32[]{:S(2)}) collective-permute-start(bf16[256,512]{0,1:T(8,128)(2,1)} %convert_element_type.502), channel_id=1, source_target_pairs={{0,2},{2,4},{4,6},{6,8},{8,10},{10,12},{12,14},{14,16},{16,18},{18... | collective-permute-start | bytes 786440 | tf_op jit(solution)/shard_map/while/body/eval_jaxpr/ppermute | solution.py:19
  597.0 16.5 %collective-permute-start.2 = (bf16[256,512]{0,1:T(8,128)(2,1)S(1)}, bf16[256,512]{0,1:T(8,128)(2,1)}, u32[]{:S(2)}, u32[]{:S(2)}) collective-permute-start(bf16[256,512]{0,1:T(8,128)(2,1)S(1)} %convert_element_type.500), channel_id=1, source_target_pairs={{0,2},{2,4},{4,6},{6,8},{8,10},{10,12},{12,14},{14,16},{16,18},{18... | collective-permute-start | bytes 786440 | tf_op jit(solution)/shard_map/while/body/eval_jaxpr/ppermute | solution.py:19
  672.8 16.7 %collective-permute-start.2 = (bf16[256,512]{0,1:T(8,128)(2,1)S(1)}, bf16[256,512]{0,1:T(8,128)(2,1)}, u32[]{:S(2)}, u32[]{:S(2)}) collective-permute-start(bf16[256,512]{0,1:T(8,128)(2,1)S(1)} %convert_element_type.500), channel_id=1, source_target_pairs={{0,2},{2,4},{4,6},{6,8},{8,10},{10,12},{12,14},{14,16},{16,18},{18... | collective-permute-start | bytes 786440 | tf_op jit(solution)/shard_map/while/body/eval_jaxpr/ppermute | solution.py:19
  674.5 16.8 %collective-permute-start.3 = (bf16[256,512]{0,1:T(8,128)(2,1)}, bf16[256,512]{0,1:T(8,128)(2,1)S(1)}, u32[]{:S(2)}, u32[]{:S(2)}) collective-permute-start(bf16[256,512]{0,1:T(8,128)(2,1)} %convert_element_type.502), channel_id=1, source_target_pairs={{0,2},{2,4},{4,6},{6,8},{8,10},{10,12},{12,14},{14,16},{16,18},{18... | collective-permute-start | bytes 786440 | tf_op jit(solution)/shard_map/while/body/eval_jaxpr/ppermute | solution.py:19
  699.9 17.4 %collective-permute-start.2 = (bf16[256,512]{0,1:T(8,128)(2,1)S(1)}, bf16[256,512]{0,1:T(8,128)(2,1)}, u32[]{:S(2)}, u32[]{:S(2)}) collective-permute-start(bf16[256,512]{0,1:T(8,128)(2,1)S(1)} %convert_element_type.500), channel_id=1, source_target_pairs={{0,2},{2,4},{4,6},{6,8},{8,10},{10,12},{12,14},{14,16},{16,18},{18... | collective-permute-start | bytes 786440 | tf_op jit(solution)/shard_map/while/body/eval_jaxpr/ppermute | solution.py:19
  702.4 16.8 %collective-permute-start.3 = (bf16[256,512]{0,1:T(8,128)(2,1)}, bf16[256,512]{0,1:T(8,128)(2,1)S(1)}, u32[]{:S(2)}, u32[]{:S(2)}) collective-permute-start(bf16[256,512]{0,1:T(8,128)(2,1)} %convert_element_type.502), channel_id=1, source_target_pairs={{0,2},{2,4},{4,6},{6,8},{8,10},{10,12},{12,14},{14,16},{16,18},{18... | collective-permute-start | bytes 786440 | tf_op jit(solution)/shard_map/while/body/eval_jaxpr/ppermute | solution.py:19
  754.2 16.6 %collective-permute-start.2 = (bf16[256,512]{0,1:T(8,128)(2,1)S(1)}, bf16[256,512]{0,1:T(8,128)(2,1)}, u32[]{:S(2)}, u32[]{:S(2)}) collective-permute-start(bf16[256,512]{0,1:T(8,128)(2,1)S(1)} %convert_element_type.500), channel_id=1, source_target_pairs={{0,2},{2,4},{4,6},{6,8},{8,10},{10,12},{12,14},{14,16},{16,18},{18... | collective-permute-start | bytes 786440 | tf_op jit(solution)/shard_map/while/body/eval_jaxpr/ppermute | solution.py:19
  779.7 143.2 %all-reduce.24.cloned.1.call-start = ((), (), s32[]{:S(2)}) async-start(), calls=%async_computation.8 | async-start | bytes 1572864 | tf_op jit(solution)/shard_map/psum | solution.py:51
  891.9 547.5 %all-reduce.22.cloned.1.call-start = ((), (), s32[]{:S(2)}) async-start(), calls=%async_computation.7 | async-start | bytes 58720256 | tf_op jit(solution)/shard_map/psum | solution.py:328
  (194 other events, 1868.9 us)
Sparse Core Ops, SparseCore 0:
  12.8 53.2 all-gather.2
  68.8 49.0 all-gather.4
  184.4 27.0 all-reduce.11
  225.1 28.5 all-reduce.13
  272.0 28.5 all-reduce.15
  314.7 28.5 all-reduce.17
  779.8 36.5 all-reduce.19
  892.0 30.8 all-reduce.23
  929.9 509.5 all-reduce.21
where the time goes:
time: 1480 us; the launch traced here: 1470 us
  waiting for transfers between devices  749 us (51%)
  starting transfers between devices  234 us (16%)
  local copies, waits for them, and re-layouts  142 us (10%)
  other arithmetic  127 us (9%)
  matrix products  109 us (7%)
  blocking collectives  67.9 us (5%)
  loops' own time  23.5 us (2%)
  between operations  16.3 us (1%)
    psum x1, waiting for transfers between devices, shards(): lax.psum((grad_query_weight, grad_key_weight, grad_value_weight, grad_out...  513 us
    ppermute x32, starting transfers between devices, shifted(): return lax.ppermute(block, axis, route)  149 us
    psum x6, waiting for transfers between devices, head_sum(): return lax.psum(values.astype(jnp.bfloat16), 'tp').astype(jnp.float32)  134 us
    ppermute x32, starting transfers between devices, shifted_2(): lax.ppermute(value, axis, [(i, (i + by) % size) for i in range(size)])  83.7 us
    psum x1, blocking collectives, shards(): lax.psum((text_key_part.reshape(text_count, width_here), text_value_part....  67.9 us
    dot_general x30, matrix products, matmul(): return jnp.dot(left, right, preferred_element_type=jnp.float32)  67 us
    all_gather x1, waiting for transfers between devices, shards(): value_piece = lax.all_gather(values, 'blk', axis=0, tiled=True)  51.8 us
    all_gather x1, waiting for transfers between devices, shards(): key_piece = lax.all_gather(keys, 'blk', axis=0, tiled=True)  44.2 us
  transfers between devices with their start and end apart: 73, of which 15 were waited for; matrix products, arithmetic and copies ran while one was open for 7% of the time, Pallas kernels for 0%

commit v1 on v0

--- a/solution.py
+++ b/solution.py
@@ -6,6 +6,18 @@
 HEAD_DIM = 64
 EPSILON = 1e-05
 NEGATIVE = -1e30
+
+
+def gather_by_bits(x, axis, dim):
+    ways, here = (lax.axis_size(axis), lax.axis_index(axis))
+    grown, reach = (x, 1)
+    while reach < ways:
+        theirs = lax.ppermute(grown, axis, [(d, d ^ reach) for d in range(ways)])
+        mine_first = jnp.concatenate([grown, theirs], axis=dim)
+        theirs_first = jnp.concatenate([theirs, grown], axis=dim)
+        grown = jnp.where(here & reach == 0, mine_first, theirs_first)
+        reach = 2 * reach
+    return grown
 
 
 def shifted(block, axis, distance):
@@ -134,7 +146,7 @@
     )
     start = jnp.int32(0)
     key_piece = lax.all_gather(keys, "blk", axis=0, tiled=True)
-    value_piece = lax.all_gather(values, "blk", axis=0, tiled=True)
+    value_piece = gather_by_bits(values, "blk", 0)
     count = key_piece.shape[0]
     key_rows = jnp.arange(count, dtype=jnp.int32)
 

time: 1480 us -> 1520 us (1.027)
  waiting for transfers between devices: 749 us -> 797 us
  local copies, waits for them, and re-layouts: 142 us -> 124 us
    ppermute x0 -> x4, waiting for transfers between devices: none -> 145 us  [gather_by_bits(): theirs = lax.ppermute(grown, axis, [(d, d ^ reach) for d in range(ways)])]
    all_gather x1 -> x0, waiting for transfers between devices: 51.8 us -> none  [shards(): value_piece = lax.all_gather(values, 'blk', axis=0, tiled=True)]
    all_gather x1, waiting for transfers between devices: 44.2 us -> 0.01 us  [shards(): key_piece = lax.all_gather(keys, 'blk', axis=0, tiled=True)]
    slice x32, local copies, waits for them, and re-layouts: 41.3 us -> 17.5 us  [key_turn(): needed = (base <= rows[-1]) & (base + row_count - 1 >= first[0])]
    unnamed x198 -> x214, local copies, waits for them, and re-layouts: 39 us -> 39.6 us
  transfers between devices with their start and end apart: 73 -> 76, of which waited for: 15 -> 15; matrix products, arithmetic and copies ran while one was open for 7% -> 8% of each run, Pallas kernels for 0% -> 0%
where the time goes in v1:
time: 1520 us; the launch traced here: 1510 us
  waiting for transfers between devices  797 us (52%)
  starting transfers between devices  236 us (16%)
  other arithmetic  140 us (9%)
  local copies, waits for them, and re-layouts  124 us (8%)
  matrix products  108 us (7%)
  blocking collectives  67.9 us (4%)
  loops' own time  23.2 us (2%)
  between operations  16.7 us (1%)
    psum x1, waiting for transfers between devices, shards(): lax.psum((grad_query_weight, grad_key_weight, grad_value_weight, grad_out...  513 us
    ppermute x32, starting transfers between devices, shifted(): return lax.ppermute(block, axis, route)  147 us
    ppermute x4, waiting for transfers between devices, gather_by_bits(): theirs = lax.ppermute(grown, axis, [(d, d ^ reach) for d in range(ways)])  145 us
    psum x6, waiting for transfers between devices, head_sum(): return lax.psum(values.astype(jnp.bfloat16), 'tp').astype(jnp.float32)  135 us
    ppermute x32, starting transfers between devices, shifted_2(): lax.ppermute(value, axis, [(i, (i + by) % size) for i in range(size)])  82.6 us
    psum x1, blocking collectives, shards(): lax.psum((text_key_part.reshape(text_count, width_here), text_value_part....  67.9 us
    dot_general x30, matrix products, matmul(): return jnp.dot(left, right, preferred_element_type=jnp.float32)  65.6 us
    while x128, local copies, waits for them, and re-layouts  40 us
  transfers between devices with their start and end apart: 76, of which 15 were waited for; matrix products, arithmetic and copies ran while one was open for 8% of the time, Pallas kernels for 0%

profile of v1, /device:TPU:0, one launch (start us, length us, event | category | flops | bytes accessed | tf_op | source)
XLA Modules:
  0.0 1513.5 jit_solution(1085477493136114271)
XLA Ops:
  18.1 15.1 %collective-permute-done.5 = bf16[512,512]{1,0:T(8,128)(2,1)} collective-permute-done((bf16[512,512]{1,0:T(8,128)(2,1)S(1)}, bf16[512,512]{1,0:T(8,128)(2,1)}, u32[]{:S(2)}, u32[]{:S(2)}) %collective-permute-start.5) | collective-permute-done | bytes 524320 | tf_op jit(solution)/shard_map/ppermute | solution.py:15
  36.7 41.4 %collective-permute-done.6 = bf16[1024,512]{1,0:T(8,128)(2,1)} collective-permute-done((bf16[1024,512]{1,0:T(8,128)(2,1)S(1)}, bf16[1024,512]{1,0:T(8,128)(2,1)}, u32[]{:S(2)}, u32[]{:S(2)}) %collective-permute-start.6) | collective-permute-done | bytes 1048608 | tf_op jit(solution)/shard_map/ppermute | solution.py:15
  86.8 87.3 %collective-permute-done.7 = bf16[2048,512]{1,0:T(8,128)(2,1)} collective-permute-done((bf16[2048,512]{1,0:T(8,128)(2,1)}, bf16[2048,512]{1,0:T(8,128)(2,1)}, u32[]{:S(2)}, u32[]{:S(2)}) %collective-permute-start.7) | collective-permute-done | bytes 2097184 | tf_op jit(solution)/shard_map/ppermute | solution.py:15
  180.0 74.0 %conditional.2 = (f32[256,8,64]{0,2,1:T(8,128)S(1)}, f32[8,256]{1,0:T(8,128)}, f32[8,256]{1,0:T(8,128)}, f32[8,256]{1,0:T(8,128)S(1)}) conditional(s32[]{:T(128)} %bitcast.13, () %tuple.58, (s32[4096]{0:T(1024)S(1)}, s32[4096]{0:T(1024)S(1)}, s32[256]{0:T(256)S(1)}, s32[256]{0:T(256)S(1)}, bf16[4096,512]{1,0:T(8,128)(2,1)}, ...), branch_computations={%region_5.6_spmd, %region_6.9_spmd} | conditional | flops 2236610560 | bytes 151881776 | solution.py:175
  205.3 15.6 %select_reduce_fusion = (f32[8,256]{1,0:T(8,128)S(1)}, f32[8,256,4096]{2,1,0:T(8,128)}) fusion(pred[256,4096]{1,0:T(8,128)(4,1)S(1)} %compare_and_fusion, bf16[256,8,64]{0,2,1:T(8,128)(2,1)S(1)} %get-tuple-element.503, bf16[4096,8,64]{0,2,1:T(8,128)(2,1)} %bitcast.126), kind=kOutput, calls=%fused_computation.2 | convolution fusion | flops 1090516992 | bytes 39067648 | tf_op jit(solution)/shard_map/cond/branch_1_fun/qhd,khd->hqk/dot_general | solution.py:157
  221.6 15.6 %fusion.7 = f32[256,8,64]{0,2,1:T(8,128)S(1)} fusion(bf16[4096,8,64]{0,2,1:T(8,128)(2,1)} %bitcast.133, f32[8,256,4096]{2,1,0:T(8,128)} %get-tuple-element.804, f32[8,256]{1,0:T(8,128)} %broadcast_maximum_fusion, pred[256,4096]{1,0:T(8,128)(4,1)S(1)} %compare_and_fusion), kind=kOutput, calls=%fused_computation.9 | convolution fusion | flops 1107296256 | bytes 39329792 | tf_op jit(solution)/shard_map/cond/branch_1_fun/hqk,khd->qhd/dot_general | solution.py:165
  237.1 16.2 %fusion.2 = f32[8,256]{1,0:T(8,128)} fusion(f32[8,256,4096]{2,1,0:T(8,128)} %get-tuple-element.804, f32[8,256]{1,0:T(8,128)} %broadcast_maximum_fusion, pred[256,4096]{1,0:T(8,128)(4,1)S(1)} %compare_and_fusion), kind=kLoop, calls=%fused_computation.3 | loop fusion | flops 33552384 | bytes 34619392 | tf_op jit(solution)/shard_map/cond/branch_1_fun/reduce_sum | solution.py:164
  262.5 22.4 %all-reduce.12.cloned.1.call-done = bf16[256,1024]{1,0:T(8,128)(2,1)} async-done(((bf16[256,1024]{1,0:T(8,128)(2,1)}), bf16[256,1024]{1,0:T(8,128)(2,1)}) %all-reduce.12.cloned.1.call-update) | async-done | bytes 524304 | tf_op jit(solution)/shard_map/psum | solution.py:63
  301.6 25.3 %all-reduce.14.cloned.1.call-done = bf16[256,1024]{1,0:T(8,128)(2,1)} async-done(((bf16[256,1024]{1,0:T(8,128)(2,1)}), bf16[256,1024]{1,0:T(8,128)(2,1)}) %all-reduce.14.cloned.1.call-update) | async-done | bytes 524304 | tf_op jit(solution)/shard_map/psum | solution.py:63
  333.4 6.6 add_convert_fusion
  358.3 15.6 %all-reduce.16.cloned.1.call-done = bf16[256,1024]{1,0:T(8,128)(2,1)} async-done(((bf16[256,1024]{1,0:T(8,128)(2,1)}), bf16[256,1024]{1,0:T(8,128)(2,1)}) %all-reduce.16.cloned.1.call-update) | async-done | bytes 524304 | tf_op jit(solution)/shard_map/psum | solution.py:63
  391.1 25.5 %all-reduce.18.cloned.1.call-done = bf16[256,1024]{1,0:T(8,128)(2,1)} async-done(((bf16[256,1024]{1,0:T(8,128)(2,1)}), bf16[256,1024]{1,0:T(8,128)(2,1)}) %all-reduce.18.cloned.1.call-update) | async-done | bytes 524304 | tf_op jit(solution)/shard_map/psum | solution.py:63
  426.6 391.5 %while.26 = (s32[]{:T(128)}, bf16[256,512]{0,1:T(8,128)(2,1)S(1)}, bf16[256,512]{0,1:T(8,128)(2,1)}, f32[256,512]{0,1:T(8,128)}, f32[256,512]{0,1:T(8,128)}, /*i...) while((s32[]{:T(128)}, bf16[256,512]{0,1:T(8,128)(2,1)S(1)}, ...), condition=%wide.region_29.30_spmd.clone, body=%wide.region_26.29_spmd.clone.sunk | while | flops 341115168 | bytes 37714808 | solution.py:306
  481.3 6.9 collective-permute-start.3
  509.2 7.1 collective-permute-start
  537.7 9.7 collective-permute-start.1
  631.0 7.0 collective-permute-start
  659.5 8.7 collective-permute-start.1
  752.7 7.0 collective-permute-start
  781.3 7.7 collective-permute-start.1
  827.8 32.9 %all-reduce.20.cloned.1.call-done = bf16[256,1024]{1,0:T(8,128)(2,1)} async-done(((bf16[256,1024]{1,0:T(8,128)(2,1)}), bf16[256,1024]{1,0:T(8,128)(2,1)}) %all-reduce.20.cloned.1.call-update) | async-done | bytes 524304 | tf_op jit(solution)/shard_map/psum | solution.py:63
  864.4 67.9 %all-reduce.25 = (bf16[128,512]{0,1:T(8,128)(2,1)S(1)}, bf16[128,512]{0,1:T(8,128)(2,1)}, f32[1024]{0:T(1024)}, f32[1024]{0:T(1024)}, f32[1024]{0:T(1024)}, /*in...) all-reduce(f32[128,512]{0,1:T(8,128)S(1)} %bitcast.142, ...), channel_id=1, replica_groups=mesh['blk'=16,'tp'=2] {'blk'}, use_global_device_ids=true, to_apply=%region_33.34 | all-reduce | flops 137216 | bytes 835584 | tf_op jit(solution)/shard_map/psum | solution.py:240
  953.7 13.5 all-reduce.24.cloned.1.call-done
  971.0 512.8 %all-reduce.22.cloned.1.call-done = (f32[1024,512]{1,0:T(8,128)}, f32[1024,512]{1,0:T(8,128)}, f32[1024,512]{1,0:T(8,128)}, f32[512,1024]{1,0:T(8,128)}, f32[102...) async-done(((f32[1024,512]{1,0:T(8,128)}, f32[1024,512]{1,0:T(8,128)}, f32[1024,512]{1,0:T(8,128)}, f32[512,1024]{1,0:T(8,128)}, ...) | async-done | bytes 29360144 | tf_op jit(solution)/shard_map/psum | solution.py:340
  (747 shorter events, 510.6 us)
Async XLA Ops:
  7.3 172.7 %all-gather.2.cloned.1.call-start = ((), (), s32[]{:S(2)}) async-start(), calls=%async_computation | async-start | bytes 4456448 | tf_op jit(solution)/shard_map/all_gather | solution.py:148
  12.7 272.2 %all-reduce.12.cloned.1.call-start = ((), (), s32[]{:S(2)}) async-start(), calls=%async_computation.1 | async-start | bytes 1048576 | tf_op jit(solution)/shard_map/psum | solution.py:63
  15.2 18.1 %collective-permute-start.5 = (bf16[512,512]{1,0:T(8,128)(2,1)S(1)}, bf16[512,512]{1,0:T(8,128)(2,1)}, u32[]{:S(2)}, u32[]{:S(2)}) collective-permute-start(bf16[512,512]{1,0:T(8,128)(2,1)S(1)} %maximum_select_fusion.2), channel_id=1, source_target_pairs={{0,4},{2,6},{4,0},{6,2},{8,12},{10,14},{12,8},{14,10},{16,20},{18,... | collective-permute-start | bytes 1572872 | tf_op jit(solution)/shard_map/ppermute | solution.py:15
  34.9 43.3 %collective-permute-start.6 = (bf16[1024,512]{1,0:T(8,128)(2,1)S(1)}, bf16[1024,512]{1,0:T(8,128)(2,1)}, u32[]{:S(2)}, u32[]{:S(2)}) collective-permute-start(bf16[1024,512]{1,0:T(8,128)(2,1)S(1)} %maximum_select_fusion.1), channel_id=1, source_target_pairs={{0,8},{2,10},{4,12},{6,14},{8,0},{10,2},{12,4},{14,6},{16,24},{18,... | collective-permute-start | bytes 3145736 | tf_op jit(solution)/shard_map/ppermute | solution.py:15
  81.7 92.4 %collective-permute-start.7 = (bf16[2048,512]{1,0:T(8,128)(2,1)}, bf16[2048,512]{1,0:T(8,128)(2,1)}, u32[]{:S(2)}, u32[]{:S(2)}) collective-permute-start(bf16[2048,512]{1,0:T(8,128)(2,1)} %maximum_select_fusion), channel_id=1, source_target_pairs={{0,16},{2,18},{4,20},{6,22},{8,24},{10,26},{12,28},{14,30},{16,0},... | collective-permute-start | bytes 6291464 | tf_op jit(solution)/shard_map/ppermute | solution.py:15
  257.5 69.4 %all-reduce.14.cloned.1.call-start = ((), (), s32[]{:S(2)}) async-start(), calls=%async_computation.2 | async-start | bytes 1048576 | tf_op jit(solution)/shard_map/psum | solution.py:63
  298.2 75.6 %all-reduce.16.cloned.1.call-start = ((), (), s32[]{:S(2)}) async-start(), calls=%async_computation.3 | async-start | bytes 1048576 | tf_op jit(solution)/shard_map/psum | solution.py:63
  345.0 71.6 %all-reduce.18.cloned.1.call-start = ((), (), s32[]{:S(2)}) async-start(), calls=%async_computation.4 | async-start | bytes 1048576 | tf_op jit(solution)/shard_map/psum | solution.py:63
  387.9 472.8 %all-reduce.20.cloned.1.call-start = ((), (), s32[]{:S(2)}) async-start(), calls=%async_computation.5 | async-start | bytes 1048576 | tf_op jit(solution)/shard_map/psum | solution.py:63
  478.3 17.1 %collective-permute-start.2 = (bf16[256,512]{0,1:T(8,128)(2,1)S(1)}, bf16[256,512]{0,1:T(8,128)(2,1)}, u32[]{:S(2)}, u32[]{:S(2)}) collective-permute-start(bf16[256,512]{0,1:T(8,128)(2,1)S(1)} %convert_element_type.501), channel_id=1, source_target_pairs={{0,2},{2,4},{4,6},{6,8},{8,10},{10,12},{12,14},{14,16},{16,18},{18... | collective-permute-start | bytes 786440 | tf_op jit(solution)/shard_map/while/body/eval_jaxpr/ppermute | solution.py:31
  504.3 17.1 %collective-permute-start.2 = (bf16[256,512]{0,1:T(8,128)(2,1)S(1)}, bf16[256,512]{0,1:T(8,128)(2,1)}, u32[]{:S(2)}, u32[]{:S(2)}) collective-permute-start(bf16[256,512]{0,1:T(8,128)(2,1)S(1)} %convert_element_type.501), channel_id=1, source_target_pairs={{0,2},{2,4},{4,6},{6,8},{8,10},{10,12},{12,14},{14,16},{16,18},{18... | collective-permute-start | bytes 786440 | tf_op jit(solution)/shard_map/while/body/eval_jaxpr/ppermute | solution.py:31
  506.8 16.5 %collective-permute-start.3 = (bf16[256,512]{0,1:T(8,128)(2,1)}, bf16[256,512]{0,1:T(8,128)(2,1)S(1)}, u32[]{:S(2)}, u32[]{:S(2)}) collective-permute-start(bf16[256,512]{0,1:T(8,128)(2,1)} %convert_element_type.503), channel_id=1, source_target_pairs={{0,2},{2,4},{4,6},{6,8},{8,10},{10,12},{12,14},{14,16},{16,18},{18... | collective-permute-start | bytes 786440 | tf_op jit(solution)/shard_map/while/body/eval_jaxpr/ppermute | solution.py:31
  530.4 17.1 %collective-permute-start.2 = (bf16[256,512]{0,1:T(8,128)(2,1)S(1)}, bf16[256,512]{0,1:T(8,128)(2,1)}, u32[]{:S(2)}, u32[]{:S(2)}) collective-permute-start(bf16[256,512]{0,1:T(8,128)(2,1)S(1)} %convert_element_type.501), channel_id=1, source_target_pairs={{0,2},{2,4},{4,6},{6,8},{8,10},{10,12},{12,14},{14,16},{16,18},{18... | collective-permute-start | bytes 786440 | tf_op jit(solution)/shard_map/while/body/eval_jaxpr/ppermute | solution.py:31
  532.8 16.5 %collective-permute-start.3 = (bf16[256,512]{0,1:T(8,128)(2,1)}, bf16[256,512]{0,1:T(8,128)(2,1)S(1)}, u32[]{:S(2)}, u32[]{:S(2)}) collective-permute-start(bf16[256,512]{0,1:T(8,128)(2,1)} %convert_element_type.503), channel_id=1, source_target_pairs={{0,2},{2,4},{4,6},{6,8},{8,10},{10,12},{12,14},{14,16},{16,18},{18... | collective-permute-start | bytes 786440 | tf_op jit(solution)/shard_map/while/body/eval_jaxpr/ppermute | solution.py:31
  600.1 17.1 %collective-permute-start.2 = (bf16[256,512]{0,1:T(8,128)(2,1)S(1)}, bf16[256,512]{0,1:T(8,128)(2,1)}, u32[]{:S(2)}, u32[]{:S(2)}) collective-permute-start(bf16[256,512]{0,1:T(8,128)(2,1)S(1)} %convert_element_type.501), channel_id=1, source_target_pairs={{0,2},{2,4},{4,6},{6,8},{8,10},{10,12},{12,14},{14,16},{16,18},{18... | collective-permute-start | bytes 786440 | tf_op jit(solution)/shard_map/while/body/eval_jaxpr/ppermute | solution.py:31
  602.6 16.5 %collective-permute-start.3 = (bf16[256,512]{0,1:T(8,128)(2,1)}, bf16[256,512]{0,1:T(8,128)(2,1)S(1)}, u32[]{:S(2)}, u32[]{:S(2)}) collective-permute-start(bf16[256,512]{0,1:T(8,128)(2,1)} %convert_element_type.503), channel_id=1, source_target_pairs={{0,2},{2,4},{4,6},{6,8},{8,10},{10,12},{12,14},{14,16},{16,18},{18... | collective-permute-start | bytes 786440 | tf_op jit(solution)/shard_map/while/body/eval_jaxpr/ppermute | solution.py:31
  626.2 17.1 %collective-permute-start.2 = (bf16[256,512]{0,1:T(8,128)(2,1)S(1)}, bf16[256,512]{0,1:T(8,128)(2,1)}, u32[]{:S(2)}, u32[]{:S(2)}) collective-permute-start(bf16[256,512]{0,1:T(8,128)(2,1)S(1)} %convert_element_type.501), channel_id=1, source_target_pairs={{0,2},{2,4},{4,6},{6,8},{8,10},{10,12},{12,14},{14,16},{16,18},{18... | collective-permute-start | bytes 786440 | tf_op jit(solution)/shard_map/while/body/eval_jaxpr/ppermute | solution.py:31
  628.6 16.4 %collective-permute-start.3 = (bf16[256,512]{0,1:T(8,128)(2,1)}, bf16[256,512]{0,1:T(8,128)(2,1)S(1)}, u32[]{:S(2)}, u32[]{:S(2)}) collective-permute-start(bf16[256,512]{0,1:T(8,128)(2,1)} %convert_element_type.503), channel_id=1, source_target_pairs={{0,2},{2,4},{4,6},{6,8},{8,10},{10,12},{12,14},{14,16},{16,18},{18... | collective-permute-start | bytes 786440 | tf_op jit(solution)/shard_map/while/body/eval_jaxpr/ppermute | solution.py:31
  721.9 17.1 %collective-permute-start.2 = (bf16[256,512]{0,1:T(8,128)(2,1)S(1)}, bf16[256,512]{0,1:T(8,128)(2,1)}, u32[]{:S(2)}, u32[]{:S(2)}) collective-permute-start(bf16[256,512]{0,1:T(8,128)(2,1)S(1)} %convert_element_type.501), channel_id=1, source_target_pairs={{0,2},{2,4},{4,6},{6,8},{8,10},{10,12},{12,14},{14,16},{16,18},{18... | collective-permute-start | bytes 786440 | tf_op jit(solution)/shard_map/while/body/eval_jaxpr/ppermute | solution.py:31
  724.3 16.5 %collective-permute-start.3 = (bf16[256,512]{0,1:T(8,128)(2,1)}, bf16[256,512]{0,1:T(8,128)(2,1)S(1)}, u32[]{:S(2)}, u32[]{:S(2)}) collective-permute-start(bf16[256,512]{0,1:T(8,128)(2,1)} %convert_element_type.503), channel_id=1, source_target_pairs={{0,2},{2,4},{4,6},{6,8},{8,10},{10,12},{12,14},{14,16},{16,18},{18... | collective-permute-start | bytes 786440 | tf_op jit(solution)/shard_map/while/body/eval_jaxpr/ppermute | solution.py:31
  747.9 17.1 %collective-permute-start.2 = (bf16[256,512]{0,1:T(8,128)(2,1)S(1)}, bf16[256,512]{0,1:T(8,128)(2,1)}, u32[]{:S(2)}, u32[]{:S(2)}) collective-permute-start(bf16[256,512]{0,1:T(8,128)(2,1)S(1)} %convert_element_type.501), channel_id=1, source_target_pairs={{0,2},{2,4},{4,6},{6,8},{8,10},{10,12},{12,14},{14,16},{16,18},{18... | collective-permute-start | bytes 786440 | tf_op jit(solution)/shard_map/while/body/eval_jaxpr/ppermute | solution.py:31
  750.4 16.4 %collective-permute-start.3 = (bf16[256,512]{0,1:T(8,128)(2,1)}, bf16[256,512]{0,1:T(8,128)(2,1)S(1)}, u32[]{:S(2)}, u32[]{:S(2)}) collective-permute-start(bf16[256,512]{0,1:T(8,128)(2,1)} %convert_element_type.503), channel_id=1, source_target_pairs={{0,2},{2,4},{4,6},{6,8},{8,10},{10,12},{12,14},{14,16},{16,18},{18... | collective-permute-start | bytes 786440 | tf_op jit(solution)/shard_map/while/body/eval_jaxpr/ppermute | solution.py:31
  822.9 144.3 %all-reduce.24.cloned.1.call-start = ((), (), s32[]{:S(2)}) async-start(), calls=%async_computation.7 | async-start | bytes 1572864 | tf_op jit(solution)/shard_map/psum | solution.py:63
  936.2 547.5 %all-reduce.22.cloned.1.call-start = ((), (), s32[]{:S(2)}) async-start(), calls=%async_computation.6 | async-start | bytes 58720256 | tf_op jit(solution)/shard_map/psum | solution.py:340
  (205 other events, 2435.8 us)
Sparse Core Ops, SparseCore 0:
  12.8 63.4 all-gather.1
  257.6 27.2 all-reduce.11
  298.3 28.5 all-reduce.13
  345.2 28.5 all-reduce.15
  388.0 28.5 all-reduce.17
  823.0 37.6 all-reduce.19
  936.3 30.8 all-reduce.23
  974.2 509.5 all-reduce.21
